TPU v7x, 256 devices: a whole 4x4x8 slice. The times are simulated.
256 devices in a mesh: seq: 32 (over x, y, core), head: 8 (over z).
Axes of the slice: x: 4, y: 4, z: 8, core: 2. Of those that a mesh axis runs over, the one named last changes fastest.
Arguments:
- tokens: bfloat16 [32768, 2048], P('seq'), may hold values from -6 to 6
- norm_gain: bfloat16 [2048], replicated, may hold values from 0.099609375 to 1.8984375
- w_qkv: bfloat16 [3, 2048, 2048], P(None, None, 'head'), may hold values from -0.176776695 to 0.176776695
- mem_gate: float32 [16], P('head'), may hold values from -3 to 3
- w_out: bfloat16 [2048, 2048], P('head'), may hold values from -0.1875 to 0.1875
Outputs:
- attended: bfloat16 [32768, 2048], P('seq', 'head')
- memory_state: float32 [32, 16, 128, 128], P('seq', 'head')
All inputs are finite; a program needn't handle non-finite values.
Results may differ from a plain program's by a relative error of at most 0.01.
The roundings to bfloat16 on the way count: a program that leaves them out, or rounds other values in their place, can miss the bound.
Values may be sent and summed in bfloat16 or wider, within the bound.
A program may use at most 64 MiB of HBM per device.

v0:
```python
import jax
import jax.numpy as jnp
from jax import lax
from jax.sharding import PartitionSpec as P

HDIM = 128


def sent_together(arrays, axis, dim, along):
    columns = [a.reshape(*a.shape[:along], -1) for a in arrays]
    both = jnp.concatenate(columns, axis=along)
    result, at, gathered = (lax.all_gather(both, axis, axis=dim, tiled=True), 0, [])
    for a, column in zip(arrays, columns):
        section = result[..., at : at + column.shape[along]]
        gathered.append(section.reshape(*section.shape[:along], *a.shape[along:]))
        at += column.shape[along]
    return tuple(gathered)


def elu_one(values_in):
    return jnp.where(values_in > 0, values_in + 1.0, jnp.exp(jnp.minimum(values_in, 0.0)))


def on_device(tokens, norm_gain, w_qkv, mem_gate, w_out):
    seg_len = tokens.shape[0]
    local_heads = w_qkv.shape[2] // HDIM
    float_tokens = tokens.astype(jnp.float32)
    normed = (
        float_tokens
        * lax.rsqrt(jnp.mean(float_tokens * float_tokens, axis=-1, keepdims=True) + 1e-05)
        * norm_gain.astype(jnp.float32)
    ).astype(jnp.bfloat16)
    projected = jnp.einsum("td,cdh->cth", normed, w_qkv, preferred_element_type=jnp.float32).astype(
        jnp.bfloat16
    )
    queries = projected[0].reshape(seg_len, local_heads, HDIM)
    key_rows = projected[1].reshape(seg_len, local_heads, HDIM)
    value_rows = projected[2].reshape(seg_len, local_heads, HDIM)
    sig_keys = elu_one(key_rows.astype(jnp.float32))
    memory_delta = jnp.einsum("thd,the->hde", sig_keys, value_rows.astype(jnp.float32))
    delta_norm = jnp.sum(sig_keys, axis=0)
    zero_memory = jnp.zeros_like(memory_delta)
    zero_norm = jnp.zeros_like(delta_norm)
    my_index = lax.axis_index("seq")
    pieces = tuple(
        (
            part.astype(jnp.float32)
            for part in sent_together(
                (memory_delta[None].astype(jnp.bfloat16), delta_norm[None].astype(jnp.bfloat16)),
                "seq",
                0,
                3,
            )
        )
    )
    row_count = pieces[0].shape[0]
    keep_rows = (jnp.arange(row_count, dtype=jnp.int32) < my_index).astype(jnp.float32)
    memory_prev = zero_memory + jnp.sum(pieces[0] * keep_rows[:, None, None, None], axis=0)
    norm_prev = zero_norm + jnp.sum(pieces[1] * keep_rows[:, None, None], axis=0)
    inv_sqrt = 1.0 / HDIM**0.5
    scores = (
        jnp.einsum("qhd,khd->hqk", queries, key_rows, preferred_element_type=jnp.float32) * inv_sqrt
    )
    row_ids = lax.broadcasted_iota(jnp.int32, (seg_len, seg_len), 0)
    col_ids = lax.broadcasted_iota(jnp.int32, (seg_len, seg_len), 1)
    scores = jnp.where((col_ids <= row_ids)[None], scores, -1e30)
    weights = jax.nn.softmax(scores, axis=-1).astype(jnp.bfloat16)
    local_out = jnp.einsum("hqk,khd->qhd", weights, value_rows, preferred_element_type=jnp.float32)
    sig_q = elu_one(queries.astype(jnp.float32))
    retrieved = jnp.einsum("thd,hde->the", sig_q, memory_prev)
    normalizer = 1.0 + jnp.einsum("thd,hd->th", sig_q, norm_prev)
    gate_share = jax.nn.sigmoid(mem_gate)[None, :, None]
    mixed_out = (
        gate_share * retrieved / normalizer[..., None] + (1.0 - gate_share) * local_out
    ).astype(jnp.bfloat16)
    mixed_out = mixed_out.reshape(seg_len, local_heads * HDIM)
    weight_cols = lax.all_to_all(w_out, "head", split_axis=1, concat_axis=0, tiled=True)
    attended = jnp.dot(
        lax.all_gather(mixed_out, "head", axis=1, tiled=True),
        weight_cols,
        preferred_element_type=jnp.float32,
    ).astype(jnp.bfloat16)
    memory_state = ((memory_prev + memory_delta) / seg_len)[None]
    return (attended, memory_state)


def solution(mesh):
    placed = (P("seq", None), P(), P(None, None, "head"), P("head"), P("head", None))
    return jax.shard_map(
        on_device,
        mesh=mesh,
        in_specs=placed,
        out_specs=(P("seq", "head"), P("seq", "head", None, None)),
        check_vma=False,
    )
```

profile of v0, /device:TPU:1, one launch (start us, length us, event | category | flops | bytes accessed | tf_op | source)
XLA Modules:
  0.0 170.5 jit_solution(17933472047963940664)
XLA Ops:
  7.2 3.2 %fusion.1 = f32[1024]{0:T(1024)S(1)} fusion(bf16[1024,2048]{1,0:T(8,128)(2,1)} %param.5), kind=kLoop, calls=%fused_computation.3 | loop fusion | flops 6290432 | bytes 4198400 | tf_op jit(solution)/shard_map/reduce_sum | solution.py:30
  10.5 1.1 copy-done.1
  11.6 3.9 %fusion.17 = bf16[3,1024,256]{1,2,0:T(8,128)(2,1)S(1)} fusion(bf16[3,2048,256]{2,1,0:T(8,128)(2,1)S(1)} %copy-done, bf16[1024,2048]{1,0:T(8,128)(2,1)S(1)} %copy-done.1, f32[2048]{0:T(1024)S(1)} %convert_element_type.76, f32[1024]{0:T(1024)S(1)} %add_rsqrt_fusion), kind=kOutput, calls=%fused_computation.30 | convolution fusion | flops 3230400512 | bytes 8925184 | tf_op jit(solution)/shard_map/td,cdh->cth/dot_general | solution.py:33
  15.5 1.2 fusion.58
  16.7 0.4 fusion.32
  17.0 2.1 %copy.44 = bf16[1024,2,128]{2,0,1:T(8,128)(2,1)} copy(bf16[1024,2,128]{0,2,1:T(8,128)(2,1)} %bitcast.59) | data formatting | bytes 1048576 | tf_op jit(solution)/shard_map/reshape;squeeze | solution.py:37
  19.1 1.6 fusion.27
  20.8 0.7 copy.46
  21.5 0.2 all-gather.5.cloned.1.call-start
  21.7 2.1 %copy.47 = bf16[1024,2,128]{2,0,1:T(8,128)(2,1)} copy(bf16[1024,2,128]{0,2,1:T(8,128)(2,1)} %bitcast.61) | data formatting | bytes 1048576 | tf_op jit(solution)/shard_map/reshape;squeeze | solution.py:36
  23.8 1.3 iota_compare_fusion
  25.1 8.2 %fusion.59 = (f32[2,1024]{1,0:T(2,128)S(1)}, f32[2,1024,1024]{1,2,0:T(8,128)}) fusion(pred[1024,1024]{0,1:T(8,128)(4,1)} %iota_compare_fusion, bf16[1024,2,128]{0,2,1:T(8,128)(2,1)} %bitcast.62, bf16[1024,2,128]{0,2,1:T(8,128)(2,1)} %bitcast.60), kind=kOutput, calls=%fused_computation.78 | convolution fusion | flops 545260544 | bytes 10493952 | tf_op jit(solution)/shard_map/sub | solution.py:67
  33.2 5.3 %fusion.24 = f32[1024,2,128]{0,2,1:T(8,128)} fusion(bf16[1024,2,128]{0,2,1:T(8,128)(2,1)} %bitcast.66, f32[2,1024,1024]{1,2,0:T(8,128)} %get-tuple-element.18, f32[2,1024]{1,0:T(2,128)S(1)} %get-tuple-element.17, f32[2]{0:T(128)S(1)} %get-tuple-element.12), kind=kOutput, calls=%fused_computation.36 | convolution fusion | flops 541327360 | bytes 9969672 | tf_op jit(solution)/shard_map/hqk,khd->qhd/dot_general | solution.py:68
  38.5 36.3 %all-gather.3.cloned.1.call-done = bf16[32,2,128,129]{2,1,3,0:T(2,128)(2,1)} async-done(((bf16[1,2,128,129]{2,1,3,0:T(2,128)(2,1)}), bf16[32,2,128,129]{2,1,3,0:T(2,128)(2,1)}) %all-gather.3.cloned.1.call-update) | async-done | bytes 2113552 | tf_op jit(solution)/shard_map/all_gather | solution.py:12
  74.8 0.8 fusion.48
  75.6 1.4 fusion.36
  77.0 3.9 %multiply_reduce_fusion = f32[2,128,128]{1,0,2:T(2,128)S(1)} fusion(f32[32]{0:T(128)S(1)} %compare_convert_fusion, bf16[32,2,128,129]{2,1,3,0:T(2,128)(2,1)} %all-gather.3.cloned.1.call-done), kind=kLoop, calls=%fused_computation.15 | loop fusion | flops 3112960 | bytes 2228352 | tf_op jit(solution)/shard_map/reduce_sum | solution.py:58
  80.9 2.7 %fusion.25 = bf16[1024,2,128]{0,2,1:T(8,128)(2,1)} fusion(f32[1024,2,128]{0,2,1:T(8,128)} %fusion.24, bf16[1024,2,128]{2,0,1:T(8,128)(2,1)} %copy.47, f32[1024,2]{0,1:T(2,128)S(1)} %fusion.49, f32[2]{0:T(128)S(1)} %get-tuple-element.13, f32[2,128,128]{1,0,2:T(2,128)S(1)} %multiply_reduce_fusion), kind=kOutput, calls=%fused_computation.37 | convolution fusion | flops 69468160 | bytes 2236424 | tf_op jit(solution)/shard_map/thd,hde->the/dot_general | solution.py:70
  83.6 2.3 %copy.52 = bf16[256,2048]{0,1:T(8,128)(2,1)} copy(bf16[256,2048]{1,0:T(8,128)(2,1)} %param.9) | data formatting | bytes 2097152 | tf_op args[4]
  85.9 46.3 %all_to_all.19 = bf16[256,8,256]{0,2,1:T(8,128)(2,1)} all-to-all(bf16[256,8,256]{0,2,1:T(8,128)(2,1)} %bitcast.58), channel_id=1, replica_groups=mesh['seq'=32,'head'=8] {'head'}, dimensions={1} | all-to-all | bytes 2097152 | tf_op jit(solution)/shard_map/all_to_all | solution.py:77
  132.2 2.3 %copy.53 = bf16[8,256,256]{2,1,0:T(8,128)(2,1)} copy(bf16[8,256,256]{1,2,0:T(8,128)(2,1)} %bitcast.57) | data formatting | bytes 2097152 | tf_op jit(solution)/shard_map/all_to_all | solution.py:77
  134.6 0.8 copy.55
  135.3 23.8 %all-gather.5.cloned.1.call-done = bf16[1024,2048]{0,1:T(8,128)(2,1)} async-done(((bf16[1024,256]{0,1:T(8,128)(2,1)}), bf16[1024,2048]{0,1:T(8,128)(2,1)}) %all-gather.5.cloned.1.call-update) | async-done | bytes 4194320 | tf_op jit(solution)/shard_map/all_gather | solution.py:79
  159.1 4.6 %convolution_convert_fusion = bf16[1024,256]{1,0:T(8,128)(2,1)} fusion(bf16[1024,2048]{0,1:T(8,128)(2,1)} %all-gather.5.cloned.1.call-done, bf16[2048,256]{1,0:T(8,128)(2,1)} %bitcast.63), kind=kOutput, calls=%fused_computation.38 | convolution fusion | flops 1074003968 | bytes 5767168 | tf_op jit(solution)/shard_map/dot_general | solution.py:78
  (19 shorter events, 0.2 us)
Async XLA Ops:
  7.2 3.3 %copy-start = (bf16[3,2048,256]{2,1,0:T(8,128)(2,1)S(1)}, bf16[3,2048,256]{2,1,0:T(8,128)(2,1)}, u32[]{:S(2)}) copy-start(bf16[3,2048,256]{2,1,0:T(8,128)(2,1)} %param.7) | copy-start | bytes 9437188
  7.2 3.3 %copy-start.2 = (bf16[2048]{0:T(1024)(128)(2,1)S(1)}, bf16[2048]{0:T(1024)(128)(2,1)}, u32[]{:S(2)}) copy-start(bf16[2048]{0:T(1024)(128)(2,1)} %param.6) | copy-start | bytes 12292
  7.2 67.6 %all-gather.3.cloned.1.call-start = ((), (), s32[]{:S(2)}) async-start(), calls=%async_computation.1 | async-start | bytes 2179584 | tf_op jit(solution)/shard_map/all_gather | solution.py:12
  7.2 4.4 %copy-start.1 = (bf16[1024,2048]{1,0:T(8,128)(2,1)S(1)}, bf16[1024,2048]{1,0:T(8,128)(2,1)}, u32[]{:S(2)}) copy-start(bf16[1024,2048]{1,0:T(8,128)(2,1)} %param.5) | copy-start | bytes 12582916
  15.5 9.6 %copy-start.3 = (f32[2]{0:T(128)S(1)}, f32[2]{0:T(128)}, u32[]{:S(2)}) copy-start(f32[2]{0:T(128)} %param.8) | copy-start | bytes 28
  21.5 137.7 %all-gather.5.cloned.1.call-start = ((), (), s32[]{:S(2)}) async-start(), calls=%async_computation.2 | async-start | bytes 4718592 | tf_op jit(solution)/shard_map/all_gather | solution.py:79
Sparse Core Ops, SparseCore 0:
  21.6 53.1 all-gather.2
  83.7 75.3 all-gather.4
where the time goes:
time: 171 us
  waiting for transfers between devices  60.1 us (35%)
  blocking collectives  46.3 us (27%)
  matrix products  27.6 us (16%)
  between operations  14.2 us (8%)
  local copies, waits for them, and re-layouts  12.4 us (7%)
  other arithmetic  9.68 us (6%)
    all_to_all x1, blocking collectives, on_device(): lax.all_to_all(w_out, 'head', split_axis=1, concat_axis=0, tiled=True)  46.3 us
    all_gather x1, waiting for transfers between devices, sent_together(): lax.all_gather(both, axis, axis=dim, tiled=True)  36.3 us
    all_gather x1, waiting for transfers between devices, on_device(): lax.all_gather(mixed_out, 'head', axis=1, tiled=True)  23.8 us
    sub x1, matrix products, on_device(): weights = jax.nn.softmax(scores, axis=-1).astype(jnp.bfloat16)  8.15 us
    dot_general x1, matrix products, on_device(): jnp.einsum('hqk,khd->qhd', weights, value_rows, preferred_element_type=jn...  5.3 us
    dot_general x1, matrix products, on_device(): jnp.dot(lax.all_gather(mixed_out, 'head', axis=1, tiled=True), weight_col...  4.57 us
    unnamed x10, local copies, waits for them, and re-layouts  4.15 us
    reduce_sum x1, other arithmetic, on_device(): jnp.sum(pieces[0] * keep_rows[:, None, None, None], axis=0)  3.93 us
  transfers between devices with their start and end apart: 2, of which 2 were waited for; matrix products, arithmetic and copies ran while one was open for 13% of the time, Pallas kernels for 0%

commit v1 on v0

--- a/solution.py
+++ b/solution.py
@@ -75,10 +75,17 @@
     ).astype(jnp.bfloat16)
     mixed_out = mixed_out.reshape(seg_len, local_heads * HDIM)
     weight_cols = lax.all_to_all(w_out, "head", split_axis=1, concat_axis=0, tiled=True)
+    samples_all_clear = lambda t0, axis_name, join_dim: jnp.concatenate(
+        lax.all_to_all(
+            jnp.stack([t0 for _ in range(lax.psum(1, axis_name=axis_name))], axis=0),
+            axis_name=axis_name,
+            split_axis=0,
+            concat_axis=0,
+        ),
+        axis=join_dim,
+    )
     attended = jnp.dot(
-        lax.all_gather(mixed_out, "head", axis=1, tiled=True),
-        weight_cols,
-        preferred_element_type=jnp.float32,
+        samples_all_clear(mixed_out, "head", 1), weight_cols, preferred_element_type=jnp.float32
     ).astype(jnp.bfloat16)
     memory_state = ((memory_prev + memory_delta) / seg_len)[None]
     return (attended, memory_state)

time: 171 us -> 205 us (1.20)
  waiting for transfers between devices: 60.1 us -> 119 us
  blocking collectives: 46.3 us -> 0 us
  starting transfers between devices: 0.26 us -> 15.9 us
  local copies, waits for them, and re-layouts: 12.4 us -> 17.7 us
    all_to_all x0 -> x2, waiting for transfers between devices: none -> 96.1 us  [the longest x1 96.1 us: on_device(): lax.all_to_all(jnp.stack([t0 for _ in range(lax.psum(1, axis_name=axis_na...]
    all_to_all x1 -> x0, blocking collectives: 46.3 us -> none  [on_device(): lax.all_to_all(w_out, 'head', split_axis=1, concat_axis=0, tiled=True)]
    all_gather x1 -> x0, waiting for transfers between devices: 23.8 us -> none  [on_device(): lax.all_gather(mixed_out, 'head', axis=1, tiled=True)]
    all_to_all x0 -> x2, starting transfers between devices: none -> 15.9 us  [the longest x1 9.01 us: on_device(): lax.all_to_all(w_out, 'head', split_axis=1, concat_axis=0, tiled=True)]
    all_gather x1, waiting for transfers between devices: 36.3 us -> 22.6 us  [sent_together(): lax.all_gather(both, axis, axis=dim, tiled=True)]
    another operation x0 -> x2, local copies, waits for them, and re-layouts: none -> 5.32 us  [on_device(): jnp.stack([t0 for _ in range(lax.psum(1, axis_name=axis_name))], axis=0)]
  transfers between devices with their start and end apart: 2 -> 3, of which waited for: 2 -> 2; matrix products, arithmetic and copies ran while one was open for 13% -> 16% of each run, Pallas kernels for 0% -> 0%
where the time goes in v1:
time: 205 us; the launch traced here: 204 us
  waiting for transfers between devices  119 us (58%)
  matrix products  27.6 us (13%)
  local copies, waits for them, and re-layouts  17.7 us (9%)
  starting transfers between devices  15.9 us (8%)
  between operations  14.1 us (7%)
  other arithmetic  9.73 us (5%)
    all_to_all x1, waiting for transfers between devices, on_device(): lax.all_to_all(jnp.stack([t0 for _ in range(lax.psum(1, axis_name=axis_na...  96.1 us
    all_gather x1, waiting for transfers between devices, sent_together(): lax.all_gather(both, axis, axis=dim, tiled=True)  22.6 us
    all_to_all x1, starting transfers between devices, on_device(): lax.all_to_all(w_out, 'head', split_axis=1, concat_axis=0, tiled=True)  9.01 us
    sub x1, matrix products, on_device(): weights = jax.nn.softmax(scores, axis=-1).astype(jnp.bfloat16)  8.17 us
    all_to_all x1, starting transfers between devices, on_device(): lax.all_to_all(jnp.stack([t0 for _ in range(lax.psum(1, axis_name=axis_na...  6.87 us
    dot_general x1, matrix products, on_device(): jnp.einsum('hqk,khd->qhd', weights, value_rows, preferred_element_type=jn...  5.37 us
    another operation x2, local copies, waits for them, and re-layouts, on_device(): jnp.stack([t0 for _ in range(lax.psum(1, axis_name=axis_name))], axis=0)  5.32 us
    dot_general x1, matrix products, on_device(): jnp.dot(samples_all_clear(mixed_out, 'head', 1), weight_cols, preferred_e...  4.53 us
  transfers between devices with their start and end apart: 3, of which 2 were waited for; matrix products, arithmetic and copies ran while one was open for 16% of the time, Pallas kernels for 0%

profile of v1, /device:TPU:1, one launch (start us, length us, event | category | flops | bytes accessed | tf_op | source)
XLA Modules:
  0.0 203.9 jit_solution(14127953281207876791)
XLA Ops:
  7.2 3.2 %fusion.1 = f32[1024]{0:T(1024)S(1)} fusion(bf16[1024,2048]{1,0:T(8,128)(2,1)} %param.5), kind=kLoop, calls=%fused_computation.3 | loop fusion | flops 6290432 | bytes 4198400 | tf_op jit(solution)/shard_map/reduce_sum | solution.py:30
  10.5 1.1 copy-done.1
  11.6 3.9 %fusion.19 = bf16[3,1024,256]{1,2,0:T(8,128)(2,1)S(1)} fusion(bf16[3,2048,256]{2,1,0:T(8,128)(2,1)S(1)} %copy-done, bf16[1024,2048]{1,0:T(8,128)(2,1)S(1)} %copy-done.1, f32[2048]{0:T(1024)S(1)} %convert_element_type.76, f32[1024]{0:T(1024)S(1)} %add_rsqrt_fusion), kind=kOutput, calls=%fused_computation.32 | convolution fusion | flops 3230400512 | bytes 8925184 | tf_op jit(solution)/shard_map/td,cdh->cth/dot_general | solution.py:33
  15.5 1.2 fusion.67
  17.0 2.0 copy.39
  19.0 1.6 fusion.35
  21.4 2.3 %copy.48 = bf16[256,2048]{0,1:T(8,128)(2,1)} copy(bf16[256,2048]{1,0:T(8,128)(2,1)} %param.9) | data formatting | bytes 2097152 | tf_op args[4]
  23.7 2.3 %copy.49 = bf16[256,8,256]{2,0,1:T(8,128)(2,1)} copy(bf16[256,8,256]{0,2,1:T(8,128)(2,1)} %bitcast.67) | data formatting | bytes 2097152 | tf_op jit(solution)/shard_map/all_to_all | solution.py:77
  26.0 9.0 %all-to-all-start.1 = ((bf16[256,8,256]{2,0,1:T(8,128)(2,1)}), bf16[256,8,256]{2,0,1:T(8,128)(2,1)}, u32[]{:S(2)}, u32[]{:S(2)}) async-start(bf16[256,8,256]{2,0,1:T(8,128)(2,1)} %copy.49), calls=%async_computation.1 | async-start | bytes 2097152 | tf_op jit(solution)/shard_map/all_to_all | solution.py:77
  35.0 1.3 iota_compare_fusion
  36.4 8.2 %fusion.68 = (f32[2,1024]{1,0:T(2,128)S(1)}, f32[2,1024,1024]{1,2,0:T(8,128)}) fusion(pred[1024,1024]{0,1:T(8,128)(4,1)} %iota_compare_fusion, bf16[1024,2,128]{0,2,1:T(8,128)(2,1)} %bitcast.68, bf16[1024,2,128]{0,2,1:T(8,128)(2,1)} %bitcast.71), kind=kOutput, calls=%fused_computation.82 | convolution fusion | flops 545260544 | bytes 10493952 | tf_op jit(solution)/shard_map/sub | solution.py:67
  44.5 5.4 %fusion.29 = f32[1024,2,128]{0,2,1:T(8,128)} fusion(bf16[1024,2,128]{0,2,1:T(8,128)(2,1)} %bitcast.74, f32[2,1024,1024]{1,2,0:T(8,128)} %get-tuple-element.16, f32[2,1024]{1,0:T(2,128)S(1)} %get-tuple-element.15, f32[2]{0:T(128)S(1)} %get-tuple-element.10), kind=kOutput, calls=%fused_computation.39 | convolution fusion | flops 541327360 | bytes 9969672 | tf_op jit(solution)/shard_map/hqk,khd->qhd/dot_general | solution.py:68
  49.9 2.0 %copy.42 = bf16[1024,2,128]{2,0,1:T(8,128)(2,1)} copy(bf16[1024,2,128]{0,2,1:T(8,128)(2,1)} %bitcast.69) | data formatting | bytes 1048576 | tf_op jit(solution)/shard_map/reshape;squeeze | solution.py:36
  52.0 22.6 %all-gather.2.cloned.1.call-done = bf16[32,2,128,129]{2,1,3,0:T(2,128)(2,1)} async-done(((bf16[1,2,128,129]{2,1,3,0:T(2,128)(2,1)}), bf16[32,2,128,129]{2,1,3,0:T(2,128)(2,1)}) %all-gather.2.cloned.1.call-update) | async-done | bytes 2113552 | tf_op jit(solution)/shard_map/all_gather | solution.py:12
  74.6 0.8 fusion.57
  75.4 1.4 fusion.45
  76.9 3.9 %multiply_reduce_fusion = f32[2,128,128]{1,0,2:T(2,128)S(1)} fusion(f32[32]{0:T(128)S(1)} %compare_convert_fusion, bf16[32,2,128,129]{2,1,3,0:T(2,128)(2,1)} %all-gather.2.cloned.1.call-done), kind=kLoop, calls=%fused_computation.17 | loop fusion | flops 3112960 | bytes 2228352 | tf_op jit(solution)/shard_map/reduce_sum | solution.py:58
  80.8 2.6 %fusion.30 = bf16[1024,2,128]{0,2,1:T(8,128)(2,1)} fusion(f32[1024,2,128]{0,2,1:T(8,128)} %fusion.29, bf16[1024,2,128]{2,0,1:T(8,128)(2,1)} %copy.42, f32[1024,2]{0,1:T(2,128)S(1)} %fusion.58, f32[2]{0:T(128)S(1)} %get-tuple-element.11, f32[2,128,128]{1,0,2:T(2,128)S(1)} %multiply_reduce_fusion), kind=kOutput, calls=%fused_computation.40 | convolution fusion | flops 69468160 | bytes 2236424 | tf_op jit(solution)/shard_map/thd,hde->the/dot_general | solution.py:70
  83.4 2.0 %copy.47 = bf16[1024,256]{1,0:T(8,128)(2,1)} copy(bf16[1024,256]{0,1:T(8,128)(2,1)} %bitcast.72) | data formatting | bytes 1048576 | tf_op jit(solution)/shard_map/stack;reshape | solution.py:80
  85.5 3.3 %stack.3 = bf16[8,1024,256]{2,1,0:T(8,128)(2,1)} broadcast(bf16[1024,256]{1,0:T(8,128)(2,1)} %copy.47), dimensions={1,2} | broadcast | bytes 4718592 | tf_op jit(solution)/shard_map/stack | solution.py:80
  88.8 6.9 %all-to-all-start = ((bf16[8,1024,256]{2,1,0:T(8,128)(2,1)}), bf16[8,1024,256]{2,1,0:T(8,128)(2,1)}, u32[]{:S(2)}, u32[]{:S(2)}) async-start(bf16[8,1024,256]{2,1,0:T(8,128)(2,1)} %stack.3), calls=%async_computation | async-start | bytes 8388608 | tf_op jit(solution)/shard_map/all_to_all | solution.py:79
  95.7 0.8 copy.51
  96.4 96.1 %all-to-all-done = bf16[8,1024,256]{2,1,0:T(8,128)(2,1)} async-done(((bf16[8,1024,256]{2,1,0:T(8,128)(2,1)}), bf16[8,1024,256]{2,1,0:T(8,128)(2,1)}, u32[]{:S(2)}, u32[]{:S(2)}) %all-to-all-start) | async-done | bytes 4194336 | tf_op jit(solution)/shard_map/all_to_all | solution.py:79
  192.5 4.5 %fusion.31 = bf16[1024,256]{1,0:T(8,128)(2,1)} fusion(bf16[8,1024,256]{2,1,0:T(8,128)(2,1)} %all-to-all-done, bf16[256,8,256]{2,0,1:T(8,128)(2,1)} %all-to-all-done.1), kind=kOutput, calls=%fused_computation.41 | convolution fusion | flops 1074003968 | bytes 5767168 | tf_op jit(solution)/shard_map/dot_general | solution.py:87
  (21 shorter events, 1.2 us)
Async XLA Ops:
  7.2 3.3 %copy-start = (bf16[3,2048,256]{2,1,0:T(8,128)(2,1)S(1)}, bf16[3,2048,256]{2,1,0:T(8,128)(2,1)}, u32[]{:S(2)}) copy-start(bf16[3,2048,256]{2,1,0:T(8,128)(2,1)} %param.7) | copy-start | bytes 9437188
  7.2 3.3 %copy-start.2 = (bf16[2048]{0:T(1024)(128)(2,1)S(1)}, bf16[2048]{0:T(1024)(128)(2,1)}, u32[]{:S(2)}) copy-start(bf16[2048]{0:T(1024)(128)(2,1)} %param.6) | copy-start | bytes 12292
  7.2 67.4 %all-gather.2.cloned.1.call-start = ((), (), s32[]{:S(2)}) async-start(), calls=%async_computation.2 | async-start | bytes 2179584 | tf_op jit(solution)/shard_map/all_gather | solution.py:12
  7.2 4.4 %copy-start.1 = (bf16[1024,2048]{1,0:T(8,128)(2,1)S(1)}, bf16[1024,2048]{1,0:T(8,128)(2,1)}, u32[]{:S(2)}) copy-start(bf16[1024,2048]{1,0:T(8,128)(2,1)} %param.5) | copy-start | bytes 12582916
  20.7 15.7 %copy-start.3 = (f32[2]{0:T(128)S(1)}, f32[2]{0:T(128)}, u32[]{:S(2)}) copy-start(f32[2]{0:T(128)} %param.8) | copy-start | bytes 28
  26.0 59.5 %all-to-all-start.1 = ((bf16[256,8,256]{2,0,1:T(8,128)(2,1)}), bf16[256,8,256]{2,0,1:T(8,128)(2,1)}, u32[]{:S(2)}, u32[]{:S(2)}) async-start(bf16[256,8,256]{2,0,1:T(8,128)(2,1)} %copy.49), calls=%async_computation.1 | async-start | bytes 2097152 | tf_op jit(solution)/shard_map/all_to_all | solution.py:77
  88.8 103.7 %all-to-all-start = ((bf16[8,1024,256]{2,1,0:T(8,128)(2,1)}), bf16[8,1024,256]{2,1,0:T(8,128)(2,1)}, u32[]{:S(2)}, u32[]{:S(2)}) async-start(bf16[8,1024,256]{2,1,0:T(8,128)(2,1)} %stack.3), calls=%async_computation | async-start | bytes 8388608 | tf_op jit(solution)/shard_map/all_to_all | solution.py:79
Sparse Core Ops, SparseCore 0:
  21.6 52.9 all-gather.1
